TPU v7x, 256 devices: a whole 4x4x8 slice. The times are simulated.
256 devices in a mesh: wide: 32 (over x, y, core), narrow: 8 (over z).
Axes of the slice: x: 4, y: 4, z: 8, core: 2. Of those that a mesh axis runs over, the one named last changes fastest.
Arguments:
- residual: bfloat16 [8192, 4608], P('wide'), may hold values from -6 to 6
- pre_gain: bfloat16 [4608], replicated, may hold values from 0.5 to 1.5
- query_weight: bfloat16 [4608, 4096], P('wide', 'narrow'), may hold values from -0.09375 to 0.09375
- key_weight: bfloat16 [4608, 2048], P('wide', 'narrow'), may hold values from -0.09375 to 0.09375
- value_weight: bfloat16 [4608, 2048], P('wide', 'narrow'), may hold values from -0.09375 to 0.09375
- output_weight: bfloat16 [4096, 4608], P('narrow', 'wide'), may hold values from -1 to 1
- adapter_down: bfloat16 [4608, 768], P('wide', 'narrow'), may hold values from -0.09375 to 0.09375
- adapter_up_query: bfloat16 [256, 4096], P(None, 'narrow'), may hold values from -1.5 to 1.5
- adapter_up_key: bfloat16 [256, 2048], P(None, 'narrow'), may hold values from -1.5 to 1.5
- adapter_up_value: bfloat16 [256, 2048], P(None, 'narrow'), may hold values from -1.5 to 1.5
- adapter_down_out: bfloat16 [4096, 256], P('narrow'), may hold values from -0.09375 to 0.09375
- adapter_up_out: bfloat16 [256, 4608], P(None, 'narrow'), may hold values from -1.5 to 1.5
- post_gain: bfloat16 [4608], P('narrow'), may hold values from 0.5 to 1.5
- sink_logits: float32 [32], P('narrow'), may hold values from -1 to 130
- prompt_lengths: int32 [4], replicated, may hold values from 1 to 4096, 8192 in all
- prompt_adapters: int32 [4], replicated, may hold values from 0 to 15
Outputs:
- layer_out: bfloat16 [8192, 4608], P('wide', 'narrow')
All inputs are finite; a program needn't handle non-finite values.
Results may differ from a plain program's by a relative error of at most 0.022.
Values may be sent and summed in bfloat16 or wider, within the bound.
A program may use at most 128 MiB of HBM per device.

v0:
```python
import jax
import jax.numpy as jnp
from jax import lax
from jax.sharding import PartitionSpec as P

HEAD_DIM = 128
ADAPTERS = 16
epsilon = 1e-06
adapter_scale = 0.5
rotary_base = 10000.0
score_scale = 1.0 / 12.0


def token_layout(prompt_lengths, count, first):
    ends = jnp.cumsum(prompt_lengths, dtype=jnp.int32)
    starts = ends - prompt_lengths
    places = first + jnp.arange(count, dtype=jnp.int32)
    member = jnp.logical_and(
        places[:, None] >= starts[None, :], places[:, None] < ends[None, :]
    ).astype(jnp.int32)
    labels = jnp.arange(prompt_lengths.shape[0], dtype=jnp.int32)
    prompt = jnp.sum(member * labels[None, :], axis=1)
    position = places - jnp.sum(member * starts[None, :], axis=1)
    return (member, prompt, position)


def rotate(values, position):
    half = values.shape[-1] // 2
    exponent = jnp.arange(half, dtype=jnp.float32) * (2.0 / values.shape[-1])
    frequency = jnp.power(jnp.float32(rotary_base), -exponent)
    angle = position.astype(jnp.float32)[:, None] * frequency[None, :]
    cosine = jnp.cos(angle)[:, None, :]
    sine = jnp.sin(angle)[:, None, :]
    first_half = values[..., :half]
    second_half = values[..., half:]
    return jnp.concatenate(
        [first_half * cosine - second_half * sine, second_half * cosine + first_half * sine],
        axis=-1,
    )


def select_codes(codes, adapter, projections, adapters):
    count = codes.shape[0]
    width = codes.shape[1] // (adapters * projections)
    shaped = codes.reshape(count, adapters, projections, width)
    onehot = (adapter[:, None] == jnp.arange(adapters, dtype=jnp.int32)[None, :]).astype(
        codes.dtype
    )
    kept = shaped * onehot[:, :, None, None]
    return [kept[:, :, slot, :].reshape(count, adapters * width) for slot in range(projections)]


def add_adapter(partial_out, adapter_cols, offset, own_width):
    current = lax.dynamic_slice_in_dim(partial_out, offset, own_width, 1)
    return lax.dynamic_update_slice_in_dim(partial_out, current + adapter_cols, offset, 1)


def per_device(
    residual,
    pre_gain,
    query_weight,
    key_weight,
    value_weight,
    output_weight,
    adapter_down,
    adapter_up_query,
    adapter_up_key,
    adapter_up_value,
    adapter_down_out,
    adapter_up_out,
    post_gain,
    sink_logits,
    prompt_lengths,
    prompt_adapters,
):
    tok_rows = residual.shape[0]
    first = lax.axis_index("wide") * tok_rows
    member, prompt, position = token_layout(prompt_lengths, tok_rows, first)
    adapter = jnp.sum(member * prompt_adapters[None, :], axis=1)
    stream = residual.astype(jnp.float32)
    scale_rows = lax.rsqrt(jnp.mean(stream * stream, axis=1, keepdims=True) + epsilon)
    normed = (stream * scale_rows * pre_gain.astype(jnp.float32)[None, :]).astype(jnp.bfloat16)
    query_cols = query_weight.shape[1]
    key_cols = key_weight.shape[1]
    pieces = (
        lax.all_gather(query_weight, "wide", axis=0, tiled=True),
        lax.all_gather(key_weight, "wide", axis=0, tiled=True),
        lax.all_gather(value_weight, "wide", axis=0, tiled=True),
        lax.all_gather(adapter_down, "wide", axis=0, tiled=True),
    )
    query_part, key_part, value_part, code_part = tuple(
        (jnp.dot(normed, piece, preferred_element_type=jnp.float32) for piece in pieces)
    )
    codes = lax.all_gather(code_part.astype(jnp.bfloat16), "narrow", axis=1, tiled=True)
    chosen = select_codes(codes, adapter, 3, ADAPTERS)
    query = query_part + adapter_scale * jnp.dot(
        chosen[0], adapter_up_query, preferred_element_type=jnp.float32
    )
    key = key_part + adapter_scale * jnp.dot(
        chosen[1], adapter_up_key, preferred_element_type=jnp.float32
    )
    value = value_part + adapter_scale * jnp.dot(
        chosen[2], adapter_up_value, preferred_element_type=jnp.float32
    )
    local_heads = query_cols // HEAD_DIM
    local_kv = key_cols // HEAD_DIM
    group = local_heads // local_kv
    queries = (
        rotate(query.reshape(tok_rows, local_heads, HEAD_DIM), position)
        .astype(jnp.bfloat16)
        .reshape(tok_rows, local_kv, group, HEAD_DIM)
    )
    keys = rotate(key.reshape(tok_rows, local_kv, HEAD_DIM), position).astype(jnp.bfloat16)
    values = value.astype(jnp.bfloat16).reshape(tok_rows, local_kv, HEAD_DIM)
    sinks = sink_logits.reshape(local_kv, group)
    own_places = first + jnp.arange(tok_rows, dtype=jnp.int32)
    start_top = jnp.broadcast_to(sinks[None, :, :], (tok_rows, local_kv, group))
    start_total = jnp.ones((tok_rows, local_kv, group), jnp.float32)
    start_sum = jnp.zeros((tok_rows, local_kv, group, HEAD_DIM), jnp.float32)
    top = start_top
    total = start_total
    summed_values = start_sum
    piece_keys = lax.all_gather(keys, "wide", axis=0, tiled=True)
    piece_values = lax.all_gather(values, "wide", axis=0, tiled=True)
    count = piece_keys.shape[0]
    unused, key_prompt, unused_position = token_layout(prompt_lengths, count, jnp.int32(0))
    key_places = jnp.arange(count, dtype=jnp.int32)
    allowed = jnp.logical_and(
        prompt[:, None] == key_prompt[None, :], own_places[:, None] >= key_places[None, :]
    )[:, None, None, :]
    scores = (
        jnp.einsum("qgjd,kgd->qgjk", queries, piece_keys, preferred_element_type=jnp.float32)
        * score_scale
    )
    scores = jnp.where(allowed, scores, -1e30)
    fresh = jnp.maximum(top, jnp.max(scores, axis=-1))
    factor = jnp.exp(top - fresh)
    weights = jnp.where(allowed, jnp.exp(scores - fresh[..., None]), 0.0)
    total = total * factor + jnp.sum(weights, axis=-1)
    update = jnp.einsum(
        "qgjk,kgd->qgjd",
        weights.astype(jnp.bfloat16),
        piece_values,
        preferred_element_type=jnp.float32,
    )
    top, total, summed_values = (fresh, total, summed_values * factor[..., None] + update)
    attended = (
        (summed_values / total[..., None])
        .reshape(tok_rows, local_heads * HEAD_DIM)
        .astype(jnp.bfloat16)
    )
    code_terms = jnp.dot(attended, adapter_down_out, preferred_element_type=jnp.float32)
    codes_out = lax.psum(code_terms.astype(jnp.bfloat16), "narrow")
    chosen_out = select_codes(codes_out, adapter, 1, ADAPTERS)[0]
    adapter_cols = adapter_scale * jnp.dot(
        chosen_out, adapter_up_out, preferred_element_type=jnp.float32
    )
    own_width = adapter_up_out.shape[1]
    offset = lax.axis_index("narrow") * own_width
    partial_out = jnp.dot(
        attended,
        lax.all_gather(output_weight, "wide", axis=1, tiled=True),
        preferred_element_type=jnp.float32,
    )
    partial_out = add_adapter(partial_out, adapter_cols, offset, own_width)
    whole = lax.psum(partial_out.astype(jnp.bfloat16), "narrow").astype(jnp.float32)
    mean_square = jnp.mean(whole * whole, axis=1)
    projected = lax.dynamic_slice_in_dim(whole, offset, own_width, 1)
    factor_rows = lax.rsqrt(mean_square + epsilon)
    own_stream = lax.dynamic_slice_in_dim(stream, offset, own_width, 1)
    mixed = own_stream + projected * factor_rows[:, None] * post_gain.astype(jnp.float32)[None, :]
    return mixed.astype(jnp.bfloat16)


def solution(mesh):
    return jax.shard_map(
        per_device,
        mesh=mesh,
        in_specs=(
            P("wide", None),
            P(),
            P("wide", "narrow"),
            P("wide", "narrow"),
            P("wide", "narrow"),
            P("narrow", "wide"),
            P("wide", "narrow"),
            P(None, "narrow"),
            P(None, "narrow"),
            P(None, "narrow"),
            P("narrow", None),
            P(None, "narrow"),
            P("narrow"),
            P("narrow"),
            P(),
            P(),
        ),
        out_specs=P("wide", "narrow"),
        check_vma=False,
    )
```

profile of v0, /device:TPU:2, one launch (start us, length us, event | category | flops | bytes accessed | tf_op | source)
XLA Modules:
  0.0 509.5 jit_solution(2858889382094123757)
XLA Ops:
  11.8 25.8 %all_gather.25 = bf16[4608,96]{1,0:T(8,128)(2,1)S(1)} all-gather(bf16[144,96]{1,0:T(8,128)(2,1)} %param.22), channel_id=1, replica_groups=mesh['wide'=32,'narrow'=8] {'wide'}, dimensions={0}, use_global_device_ids=true | all-gather | bytes 912384 | tf_op jit(solution)/shard_map/all_gather | solution.py:89
  37.6 2.4 multiply_reduce_fusion.1
  40.0 2.7 convolution_convert_fusion.1
  42.6 28.5 %all_gather.26 = bf16[256,768]{0,1:T(8,128)(2,1)S(1)} all-gather(bf16[256,96]{0,1:T(8,128)(2,1)S(1)} %convolution_convert_fusion.1), channel_id=1, replica_groups=mesh['wide'=32,'narrow'=8] {'narrow'}, dimensions={1}, use_global_device_ids=true | all-gather | bytes 442368 | tf_op jit(solution)/shard_map/all_gather | solution.py:94
  72.5 2.9 fusion.49
  76.5 1.0 copy.45
  78.5 34.0 %all-gather.13.cloned.1.call-done = bf16[4608,256]{1,0:T(8,128)(2,1)} async-done(((bf16[144,256]{1,0:T(8,128)(2,1)}), bf16[4608,256]{1,0:T(8,128)(2,1)}) %all-gather.13.cloned.1.call-update) | async-done | bytes 2359312 | tf_op jit(solution)/shard_map/all_gather | solution.py:88
  112.4 2.9 fusion.47
  115.4 0.9 fusion.24
  118.1 4.6 fusion.6
  122.8 43.2 %all-gather.11.cloned.1.call-done = bf16[4608,512]{1,0:T(8,128)(2,1)} async-done(((bf16[144,512]{1,0:T(8,128)(2,1)}), bf16[4608,512]{1,0:T(8,128)(2,1)}) %all-gather.11.cloned.1.call-update) | async-done | bytes 4718608 | tf_op jit(solution)/shard_map/all_gather | solution.py:86
  165.9 3.8 fusion.48
  169.7 1.0 fusion.11
  170.8 1.2 reshape.200
  172.5 46.5 %all-gather.9.cloned.1.call-done = bf16[8192,2,128]{2,0,1:T(8,128)(2,1)} async-done(((bf16[256,2,128]{2,0,1:T(8,128)(2,1)}), bf16[8192,2,128]{2,0,1:T(8,128)(2,1)}) %all-gather.9.cloned.1.call-update) | async-done | bytes 4194320 | tf_op jit(solution)/shard_map/all_gather | solution.py:123
  219.0 16.1 %fusion = (f32[256,2,2]{0,2,1:T(2,128)S(1)}, f32[2,8192,256,2]{2,1,3,0:T(8,128)}) fusion(pred[256,8192]{0,1:T(8,128)(4,1)} %fusion.6, bf16[256,2,2,64]{3,0,2,1:T(8,128)(2,1)S(1)} %bitcast.85, bf16[256,2,2,64]{3,0,2,1:T(8,128)(2,1)S(1)} %bitcast.84, bf16[8192,2,128]{2,0,1:T(8,128)(2,1)} %all-gather.9.cloned.1.call-done), kind=kOutput, calls=%fused_computation.2 | convolution fusion | flops 2173172736 | bytes 40112128 | tf_op jit(solution)/shard_map/qgjd,kgd->qgjk/dot_general | solution.py:132
  235.2 15.0 %fusion.1 = f32[256,2,2]{0,2,1:T(2,128)S(1)} fusion(f32[2,8192,256,2]{2,1,3,0:T(8,128)} %get-tuple-element.22, f32[256,2,2]{0,2,1:T(2,128)S(1)} %broadcast_maximum_fusion, pred[256,8192]{0,1:T(8,128)(4,1)S(1)} %copy-done.2), kind=kLoop, calls=%fused_computation.3 | loop fusion | flops 41942016 | bytes 35659776 | tf_op jit(solution)/shard_map/reduce_sum | solution.py:139
  250.3 24.1 %all-gather.15.cloned.1.call-done = bf16[8192,2,128]{0,2,1:T(8,128)(2,1)} async-done(((bf16[256,2,128]{0,2,1:T(8,128)(2,1)}), bf16[8192,2,128]{0,2,1:T(8,128)(2,1)}) %all-gather.15.cloned.1.call-update) | async-done | bytes 4194320 | tf_op jit(solution)/shard_map/all_gather | solution.py:124
  274.4 15.9 %fusion.30 = bf16[256,2,2,128]{0,3,2,1:T(8,128)(2,1)S(1)} fusion(f32[2,8192,256,2]{2,1,3,0:T(8,128)} %get-tuple-element.22, f32[256,2,2]{0,2,1:T(2,128)S(1)} %broadcast_maximum_fusion, pred[256,8192]{0,1:T(8,128)(4,1)} %fusion.6, bf16[8192,2,128]{0,2,1:T(8,128)(2,1)} %all-gather.15.cloned.1.call-done, f32[256,2,2]{0,2,1:T(2,128)S(1)} %get-tuple-element.18, ...), kind=kOutput, calls=%fused_computation.29 | convolution fusion | flops 2189819904 | bytes 40120320 | tf_op jit(solution)/shard_map/qgjk,kgd->qgjd/dot_general | solution.py:140
  290.3 0.9 convolution_convert_fusion
  291.6 36.4 %all-gather.17.cloned.1.call-done = bf16[512,4608]{0,1:T(8,128)(2,1)} async-done(((bf16[512,144]{0,1:T(8,128)(2,1)}), bf16[512,4608]{0,1:T(8,128)(2,1)}) %all-gather.17.cloned.1.call-update) | async-done | bytes 4718608 | tf_op jit(solution)/shard_map/all_gather | solution.py:162
  328.0 5.9 %fusion.52 = f32[256,4608]{1,0:T(8,128)} fusion(bf16[256,512]{0,1:T(8,128)(2,1)S(1)} %bitcast.77, bf16[512,4608]{0,1:T(8,128)(2,1)} %all-gather.17.cloned.1.call-done), kind=kOutput, calls=%fused_computation.72 | convolution fusion | flops 1207959552 | bytes 9699328 | tf_op jit(solution)/shard_map/dot_general | solution.py:160
  333.9 68.7 %all-reduce.3.cloned.1.call-done = bf16[256,256]{1,0:T(8,128)(2,1)} async-done(((bf16[256,256]{1,0:T(8,128)(2,1)}), bf16[256,256]{1,0:T(8,128)(2,1)}) %all-reduce.3.cloned.1.call-update) | async-done | bytes 131088 | tf_op jit(solution)/shard_map/psum | solution.py:153
  402.6 1.5 fusion.10
  404.2 4.5 dynamic_update_slice.3
  408.7 4.0 convert_element_type.69
  412.7 2.7 convert_element_type.58
  415.4 80.3 %all-reduce.5.cloned.1.call-done = bf16[256,4608]{1,0:T(8,128)(2,1)} async-done(((bf16[256,4608]{1,0:T(8,128)(2,1)}), bf16[256,4608]{1,0:T(8,128)(2,1)}) %all-reduce.5.cloned.1.call-update) | async-done | bytes 2359312 | tf_op jit(solution)/shard_map/psum | solution.py:166
  495.7 2.2 multiply_reduce_fusion
  497.9 2.2 convert_element_type.70
  500.1 1.6 add_convert_fusion
  501.7 0.9 copy.39
  (69 shorter events, 11.3 us)
Async XLA Ops:
  6.5 396.1 %copy-start = (bf16[256,576]{0,1:T(8,128)(2,1)S(1)}, bf16[256,576]{0,1:T(8,128)(2,1)}, u32[]{:S(2)}) copy-start(bf16[256,576]{0,1:T(8,128)(2,1)} %param.27) | copy-start | bytes 884740
  6.5 65.9 %all-gather.7.cloned.1.call-start = ((), (), s32[]{:S(2)}) async-start(), calls=%async_computation | async-start | bytes 2433024 | tf_op jit(solution)/shard_map/all_gather | solution.py:87
  7.3 105.2 %all-gather.13.cloned.1.call-start = ((), (), s32[]{:S(2)}) async-start(), calls=%async_computation.3 | async-start | bytes 2433024 | tf_op jit(solution)/shard_map/all_gather | solution.py:88
  8.0 157.9 %all-gather.11.cloned.1.call-start = ((), (), s32[]{:S(2)}) async-start(), calls=%async_computation.2 | async-start | bytes 4866048 | tf_op jit(solution)/shard_map/all_gather | solution.py:86
  8.7 210.3 %all-gather.9.cloned.1.call-start = ((), (), s32[]{:S(2)}) async-start(), calls=%async_computation.1 | async-start | bytes 4325376 | tf_op jit(solution)/shard_map/all_gather | solution.py:123
  37.6 34.9 %copy-start.1 = (bf16[256,4608]{1,0:T(8,128)(2,1)S(1)}, bf16[256,4608]{1,0:T(8,128)(2,1)}, u32[]{:S(2)}) copy-start(bf16[256,4608]{1,0:T(8,128)(2,1)} %param.16) | copy-start | bytes 7077892
  42.6 32.8 %copy-start.9 = (bf16[256,256]{1,0:T(8,128)(2,1)S(1)}, bf16[256,256]{1,0:T(8,128)(2,1)}, u32[]{:S(2)}) copy-start(bf16[256,256]{1,0:T(8,128)(2,1)} %param.24) | copy-start | bytes 393220
  76.5 40.8 %copy-start.11 = (f32[4]{0:T(128)S(1)}, f32[4]{0:T(128)}, u32[]{:S(2)}) copy-start(f32[4]{0:T(128)} %param.29) | copy-start | bytes 52
  77.6 37.7 %copy-start.4 = (bf16[256,16,1,16]{0,3,2,1:T(8,128)(2,1)S(1)}, bf16[256,16,1,16]{0,3,2,1:T(8,128)(2,1)}, u32[]{:S(2)}) copy-start(bf16[256,16,1,16]{0,3,2,1:T(8,128)(2,1)} %get-tuple-element.12) | copy-start | bytes 393220
  77.6 37.7 %copy-start.8 = (bf16[256,256]{1,0:T(8,128)(2,1)S(1)}, bf16[256,256]{1,0:T(8,128)(2,1)}, u32[]{:S(2)}) copy-start(bf16[256,256]{1,0:T(8,128)(2,1)} %param.25) | copy-start | bytes 393220
  78.4 196.0 %all-gather.15.cloned.1.call-start = ((), (), s32[]{:S(2)}) async-start(), calls=%async_computation.4 | async-start | bytes 4325376 | tf_op jit(solution)/shard_map/all_gather | solution.py:124
  116.3 211.7 %all-gather.17.cloned.1.call-start = ((), (), s32[]{:S(2)}) async-start(), calls=%async_computation.5 | async-start | bytes 4866048 | tf_op jit(solution)/shard_map/all_gather | solution.py:162
  116.8 285.8 %all-reduce.3.cloned.1.call-start = ((), (), s32[]{:S(2)}) async-start(), calls=%async_computation.6 | async-start | bytes 262144 | tf_op jit(solution)/shard_map/psum | solution.py:153
  122.8 46.9 %copy-start.5 = (bf16[256,16,1,16]{0,3,2,1:T(8,128)(2,1)S(1)}, bf16[256,16,1,16]{0,3,2,1:T(8,128)(2,1)}, u32[]{:S(2)}) copy-start(bf16[256,16,1,16]{0,3,2,1:T(8,128)(2,1)} %get-tuple-element.13) | copy-start | bytes 393220
  122.8 46.9 %copy-start.7 = (bf16[256,512]{1,0:T(8,128)(2,1)S(1)}, bf16[256,512]{1,0:T(8,128)(2,1)}, u32[]{:S(2)}) copy-start(bf16[256,512]{1,0:T(8,128)(2,1)} %param.23) | copy-start | bytes 786436
  219.0 16.2 %copy-start.2 = (pred[256,8192]{0,1:T(8,128)(4,1)S(1)}, pred[256,8192]{0,1:T(8,128)(4,1)}, u32[]{:S(2)}) copy-start(pred[256,8192]{0,1:T(8,128)(4,1)} %fusion.6) | copy-start | bytes 6291460
  274.4 15.9 %copy-start.6 = (bf16[512,256]{1,0:T(8,128)(2,1)S(1)}, bf16[512,256]{1,0:T(8,128)(2,1)}, u32[]{:S(2)}) copy-start(bf16[512,256]{1,0:T(8,128)(2,1)} %param.26) | copy-start | bytes 786436
  291.3 111.4 %copy-start.3 = (bf16[256,256]{1,0:T(8,128)(2,1)S(1)}, bf16[256,256]{1,0:T(8,128)(2,1)}, u32[]{:S(2)}) copy-start(bf16[256,256]{1,0:T(8,128)(2,1)} %copy.37) | copy-start | bytes 393220
  291.3 204.4 %all-reduce.5.cloned.1.call-start = ((), (), s32[]{:S(2)}) async-start(), calls=%async_computation.7 | async-start | bytes 4718592 | tf_op jit(solution)/shard_map/psum | solution.py:166
  412.7 2.7 copy-start.10
Sparse Core Ops, SparseCore 0:
  9.9 51.6 all-gather.6
  64.1 48.2 all-gather.12
  115.0 50.9 all-gather.10
  168.4 50.5 all-gather.8
  221.3 53.0 all-gather.14
  276.8 51.1 all-gather.16
  330.3 72.2 all-reduce.2
  412.8 82.8 all-reduce.4
where the time goes:
time: 510 us; the launch traced here: 509 us
  waiting for transfers between devices  336 us (66%)
  matrix products  54.8 us (11%)
  blocking collectives  54.3 us (11%)
  other arithmetic  39.9 us (8%)
  between operations  13.8 us (3%)
  local copies, waits for them, and re-layouts  10.1 us (2%)
    psum x1, waiting for transfers between devices, per_device(): lax.psum(partial_out.astype(jnp.bfloat16), 'narrow').astype(jnp.float32)  80.3 us
    psum x1, waiting for transfers between devices, per_device(): codes_out = lax.psum(code_terms.astype(jnp.bfloat16), 'narrow')  68.7 us
    all_gather x1, waiting for transfers between devices, per_device(): piece_keys = lax.all_gather(keys, 'wide', axis=0, tiled=True)  46.5 us
    all_gather x1, waiting for transfers between devices, per_device(): lax.all_gather(query_weight, 'wide', axis=0, tiled=True)  43.2 us
    all_gather x1, waiting for transfers between devices, per_device(): lax.all_gather(output_weight, 'wide', axis=1, tiled=True)  36.4 us
    all_gather x1, waiting for transfers between devices, per_device(): lax.all_gather(value_weight, 'wide', axis=0, tiled=True)  34 us
    all_gather x1, blocking collectives, per_device(): lax.all_gather(code_part.astype(jnp.bfloat16), 'narrow', axis=1, tiled=True)  28.5 us
    all_gather x1, blocking collectives, per_device(): lax.all_gather(adapter_down, 'wide', axis=0, tiled=True)  25.8 us
  transfers between devices with their start and end apart: 8, of which 7 were waited for; matrix products, arithmetic and copies ran while one was open for 17% of the time, Pallas kernels for 0%

commit v1 on v0

--- a/solution.py
+++ b/solution.py
@@ -120,7 +120,11 @@
     top = start_top
     total = start_total
     summed_values = start_sum
-    piece_keys = lax.all_gather(keys, "wide", axis=0, tiled=True)
+    load_the_field = lambda patch, axis_key: jnp.concatenate(
+        lax.all_to_all(jnp.stack([patch for _ in range(lax.axis_size(axis_key))]), axis_key, 0, 0),
+        axis=0,
+    )
+    piece_keys = load_the_field(keys, "wide")
     piece_values = lax.all_gather(values, "wide", axis=0, tiled=True)
     count = piece_keys.shape[0]
     unused, key_prompt, unused_position = token_layout(prompt_lengths, count, jnp.int32(0))

time: 510 us -> 485 us (0.951)
  waiting for transfers between devices: 336 us -> 298 us
  local copies, waits for them, and re-layouts: 10.1 us -> 16.7 us
  starting transfers between devices: 0.68 us -> 6.6 us
    all_gather x1 -> x0, waiting for transfers between devices: 46.5 us -> none  [per_device(): piece_keys = lax.all_gather(keys, 'wide', axis=0, tiled=True)]
    all_to_all x0 -> x1, waiting for transfers between devices: none -> 45 us  [per_device(): lax.all_to_all(jnp.stack([patch for _ in range(lax.axis_size(axis_key))])...]
    all_gather x1, waiting for transfers between devices: 0.01 us -> 36.4 us  [per_device(): lax.all_gather(key_weight, 'wide', axis=0, tiled=True)]
    all_gather x1, waiting for transfers between devices: 34 us -> 0.01 us  [per_device(): lax.all_gather(value_weight, 'wide', axis=0, tiled=True)]
    all_gather x1, waiting for transfers between devices: 43.2 us -> 11.9 us  [per_device(): lax.all_gather(query_weight, 'wide', axis=0, tiled=True)]
    all_gather x1, waiting for transfers between devices: 24.1 us -> 17.4 us  [per_device(): piece_values = lax.all_gather(values, 'wide', axis=0, tiled=True)]
    all_to_all x0 -> x1, starting transfers between devices: none -> 5.96 us  [per_device(): lax.all_to_all(jnp.stack([patch for _ in range(lax.axis_size(axis_key))])...]
  transfers between devices with their start and end apart: 8 -> 8, of which waited for: 7 -> 7; matrix products, arithmetic and copies ran while one was open for 17% -> 19% of each run, Pallas kernels for 0% -> 0%
where the time goes in v1:
time: 485 us; the launch traced here: 484 us
  waiting for transfers between devices  298 us (61%)
  matrix products  54.9 us (11%)
  blocking collectives  54.4 us (11%)
  other arithmetic  39 us (8%)
  local copies, waits for them, and re-layouts  16.7 us (3%)
  between operations  13.8 us (3%)
  starting transfers between devices  6.6 us (1%)
    psum x1, waiting for transfers between devices, per_device(): lax.psum(partial_out.astype(jnp.bfloat16), 'narrow').astype(jnp.float32)  80.1 us
    psum x1, waiting for transfers between devices, per_device(): codes_out = lax.psum(code_terms.astype(jnp.bfloat16), 'narrow')  68.6 us
    all_to_all x1, waiting for transfers between devices, per_device(): lax.all_to_all(jnp.stack([patch for _ in range(lax.axis_size(axis_key))])...  45 us
    all_gather x1, waiting for transfers between devices, per_device(): lax.all_gather(output_weight, 'wide', axis=1, tiled=True)  36.5 us
    all_gather x1, waiting for transfers between devices, per_device(): lax.all_gather(key_weight, 'wide', axis=0, tiled=True)  36.4 us
    all_gather x1, blocking collectives, per_device(): lax.all_gather(code_part.astype(jnp.bfloat16), 'narrow', axis=1, tiled=True)  28.6 us
    all_gather x1, blocking collectives, per_device(): lax.all_gather(adapter_down, 'wide', axis=0, tiled=True)  25.8 us
    all_gather x1, waiting for transfers between devices, per_device(): piece_values = lax.all_gather(values, 'wide', axis=0, tiled=True)  17.4 us
  transfers between devices with their start and end apart: 8, of which 7 were waited for; matrix products, arithmetic and copies ran while one was open for 19% of the time, Pallas kernels for 0%

profile of v1, /device:TPU:2, one launch (start us, length us, event | category | flops | bytes accessed | tf_op | source)
XLA Modules:
  0.0 483.7 jit_solution(4400907730138677800)
XLA Ops:
  11.7 25.8 %all_gather.22 = bf16[4608,96]{1,0:T(8,128)(2,1)S(1)} all-gather(bf16[144,96]{1,0:T(8,128)(2,1)} %param.22), channel_id=1, replica_groups=mesh['wide'=32,'narrow'=8] {'wide'}, dimensions={0}, use_global_device_ids=true | all-gather | bytes 912384 | tf_op jit(solution)/shard_map/all_gather | solution.py:89
  37.5 2.4 multiply_reduce_fusion.1
  39.9 2.7 convolution_convert_fusion.1
  42.6 28.6 %all_gather.23 = bf16[256,768]{0,1:T(8,128)(2,1)S(1)} all-gather(bf16[256,96]{0,1:T(8,128)(2,1)S(1)} %convolution_convert_fusion.1), channel_id=1, replica_groups=mesh['wide'=32,'narrow'=8] {'narrow'}, dimensions={1}, use_global_device_ids=true | all-gather | bytes 442368 | tf_op jit(solution)/shard_map/all_gather | solution.py:94
  71.9 2.9 fusion.46
  76.1 36.4 %all-gather.6.cloned.1.call-done = bf16[4608,256]{1,0:T(8,128)(2,1)} async-done(((bf16[144,256]{1,0:T(8,128)(2,1)}), bf16[4608,256]{1,0:T(8,128)(2,1)}) %all-gather.6.cloned.1.call-update) | async-done | bytes 2359312 | tf_op jit(solution)/shard_map/all_gather | solution.py:87
  112.5 2.9 fusion.48
  115.8 3.0 stack.2
  118.9 6.0 %all-to-all-start = ((bf16[32,256,2,128]{3,1,2,0:T(8,128)(2,1)}), bf16[32,256,2,128]{3,1,2,0:T(8,128)(2,1)}, u32[]{:S(2)}, u32[]{:S(2)}) async-start(bf16[32,256,2,128]{3,1,2,0:T(8,128)(2,1)} %stack.2), calls=%async_computation | async-start | bytes 8388608 | tf_op jit(solution)/shard_map/all_to_all | solution.py:124
  126.9 4.7 fusion.6
  131.6 45.0 %all-to-all-done = bf16[32,256,2,128]{3,1,2,0:T(8,128)(2,1)} async-done(((bf16[32,256,2,128]{3,1,2,0:T(8,128)(2,1)}), bf16[32,256,2,128]{3,1,2,0:T(8,128)(2,1)}, u32[]{:S(2)}, u32[]{:S(2)}) %all-to-all-start) | async-done | bytes 4194336 | tf_op jit(solution)/shard_map/all_to_all | solution.py:124
  176.6 5.1 %copy.45 = bf16[32,256,2,128]{3,1,0,2:T(8,128)(2,1)} copy(bf16[32,256,2,128]{3,1,2,0:T(8,128)(2,1)} %all-to-all-done) | data formatting | bytes 8388608 | tf_op jit(solution)/shard_map/all_to_all | solution.py:124
  181.6 11.9 %all-gather.8.cloned.1.call-done = bf16[4608,512]{1,0:T(8,128)(2,1)} async-done(((bf16[144,512]{1,0:T(8,128)(2,1)}), bf16[4608,512]{1,0:T(8,128)(2,1)}) %all-gather.8.cloned.1.call-update) | async-done | bytes 4718608 | tf_op jit(solution)/shard_map/all_gather | solution.py:86
  193.5 3.8 fusion.47
  197.4 1.1 fusion.9
  198.4 1.2 reshape.211
  200.2 16.1 %fusion = (f32[256,2,2]{0,2,1:T(2,128)S(1)}, f32[2,8192,256,2]{2,1,3,0:T(8,128)}) fusion(pred[256,8192]{0,1:T(8,128)(4,1)} %fusion.6, bf16[8192,2,128,1]{2,0,3,1:T(8,128)(2,1)} %bitcast.74, bf16[256,2,2,64]{3,0,2,1:T(8,128)(2,1)S(1)} %bitcast.84, bf16[256,2,2,64]{3,0,2,1:T(8,128)(2,1)S(1)} %bitcast.85), kind=kOutput, calls=%fused_computation.2 | convolution fusion | flops 2173172736 | bytes 40112128 | tf_op jit(solution)/shard_map/qgjd,kgd->qgjk/dot_general | solution.py:136
  216.4 15.0 %fusion.1 = f32[256,2,2]{0,2,1:T(2,128)S(1)} fusion(f32[2,8192,256,2]{2,1,3,0:T(8,128)} %get-tuple-element.20, f32[256,2,2]{0,2,1:T(2,128)S(1)} %broadcast_maximum_fusion, pred[256,8192]{0,1:T(8,128)(4,1)S(1)} %copy-done.2), kind=kLoop, calls=%fused_computation.3 | loop fusion | flops 41942016 | bytes 35659776 | tf_op jit(solution)/shard_map/reduce_sum | solution.py:143
  231.5 17.4 %all-gather.12.cloned.1.call-done = bf16[8192,2,128]{0,2,1:T(8,128)(2,1)} async-done(((bf16[256,2,128]{0,2,1:T(8,128)(2,1)}), bf16[8192,2,128]{0,2,1:T(8,128)(2,1)}) %all-gather.12.cloned.1.call-update) | async-done | bytes 4194320 | tf_op jit(solution)/shard_map/all_gather | solution.py:128
  248.9 16.0 %fusion.28 = bf16[256,2,2,128]{0,3,2,1:T(8,128)(2,1)S(1)} fusion(f32[2,8192,256,2]{2,1,3,0:T(8,128)} %get-tuple-element.20, f32[256,2,2]{0,2,1:T(2,128)S(1)} %broadcast_maximum_fusion, pred[256,8192]{0,1:T(8,128)(4,1)} %fusion.6, bf16[8192,2,128]{0,2,1:T(8,128)(2,1)} %all-gather.12.cloned.1.call-done, f32[256,2,2]{0,2,1:T(2,128)S(1)} %get-tuple-element.16, ...), kind=kOutput, calls=%fused_computation.27 | convolution fusion | flops 2189819904 | bytes 40120320 | tf_op jit(solution)/shard_map/qgjk,kgd->qgjd/dot_general | solution.py:144
  264.9 0.9 convolution_convert_fusion
  266.1 36.5 %all-gather.14.cloned.1.call-done = bf16[512,4608]{0,1:T(8,128)(2,1)} async-done(((bf16[512,144]{0,1:T(8,128)(2,1)}), bf16[512,4608]{0,1:T(8,128)(2,1)}) %all-gather.14.cloned.1.call-update) | async-done | bytes 4718608 | tf_op jit(solution)/shard_map/all_gather | solution.py:166
  302.6 5.9 %fusion.50 = f32[256,4608]{1,0:T(8,128)} fusion(bf16[256,512]{0,1:T(8,128)(2,1)S(1)} %bitcast.77, bf16[512,4608]{0,1:T(8,128)(2,1)} %all-gather.14.cloned.1.call-done), kind=kOutput, calls=%fused_computation.70 | convolution fusion | flops 1207959552 | bytes 9699328 | tf_op jit(solution)/shard_map/dot_general | solution.py:164
  308.5 68.6 %all-reduce.3.cloned.1.call-done = bf16[256,256]{1,0:T(8,128)(2,1)} async-done(((bf16[256,256]{1,0:T(8,128)(2,1)}), bf16[256,256]{1,0:T(8,128)(2,1)}) %all-reduce.3.cloned.1.call-update) | async-done | bytes 131088 | tf_op jit(solution)/shard_map/psum | solution.py:157
  377.1 1.5 fusion.8
  378.6 4.5 dynamic_update_slice.3
  383.1 4.0 convert_element_type.71
  387.2 2.7 convert_element_type.60
  389.9 80.1 %all-reduce.5.cloned.1.call-done = bf16[256,4608]{1,0:T(8,128)(2,1)} async-done(((bf16[256,4608]{1,0:T(8,128)(2,1)}), bf16[256,4608]{1,0:T(8,128)(2,1)}) %all-reduce.5.cloned.1.call-update) | async-done | bytes 2359312 | tf_op jit(solution)/shard_map/psum | solution.py:170
  470.0 2.2 multiply_reduce_fusion
  472.2 2.2 convert_element_type.72
  474.4 1.6 add_convert_fusion
  (68 shorter events, 11.5 us)
Async XLA Ops:
  6.5 370.6 %copy-start = (bf16[256,576]{0,1:T(8,128)(2,1)S(1)}, bf16[256,576]{0,1:T(8,128)(2,1)}, u32[]{:S(2)}) copy-start(bf16[256,576]{0,1:T(8,128)(2,1)} %param.27) | copy-start | bytes 884740
  6.5 65.3 %all-gather.10.cloned.1.call-start = ((), (), s32[]{:S(2)}) async-start(), calls=%async_computation.3 | async-start | bytes 2433024 | tf_op jit(solution)/shard_map/all_gather | solution.py:88
  7.3 105.2 %all-gather.6.cloned.1.call-start = ((), (), s32[]{:S(2)}) async-start(), calls=%async_computation.1 | async-start | bytes 2433024 | tf_op jit(solution)/shard_map/all_gather | solution.py:87
  8.0 185.5 %all-gather.8.cloned.1.call-start = ((), (), s32[]{:S(2)}) async-start(), calls=%async_computation.2 | async-start | bytes 4866048 | tf_op jit(solution)/shard_map/all_gather | solution.py:86
  8.7 240.2 %all-gather.12.cloned.1.call-start = ((), (), s32[]{:S(2)}) async-start(), calls=%async_computation.4 | async-start | bytes 4325376 | tf_op jit(solution)/shard_map/all_gather | solution.py:128
  37.5 34.4 %copy-start.1 = (bf16[256,4608]{1,0:T(8,128)(2,1)S(1)}, bf16[256,4608]{1,0:T(8,128)(2,1)}, u32[]{:S(2)}) copy-start(bf16[256,4608]{1,0:T(8,128)(2,1)} %param.16) | copy-start | bytes 7077892
  42.6 32.3 %copy-start.7 = (bf16[256,256]{1,0:T(8,128)(2,1)S(1)}, bf16[256,256]{1,0:T(8,128)(2,1)}, u32[]{:S(2)}) copy-start(bf16[256,256]{1,0:T(8,128)(2,1)} %param.25) | copy-start | bytes 393220
  74.8 40.6 %copy-start.8 = (bf16[256,256]{1,0:T(8,128)(2,1)S(1)}, bf16[256,256]{1,0:T(8,128)(2,1)}, u32[]{:S(2)}) copy-start(bf16[256,256]{1,0:T(8,128)(2,1)} %param.24) | copy-start | bytes 393220
  118.9 7.0 %copy-start.10 = (f32[4]{0:T(128)S(1)}, f32[4]{0:T(128)}, u32[]{:S(2)}) copy-start(f32[4]{0:T(128)} %param.29) | copy-start | bytes 52
  118.9 57.7 %all-to-all-start = ((bf16[32,256,2,128]{3,1,2,0:T(8,128)(2,1)}), bf16[32,256,2,128]{3,1,2,0:T(8,128)(2,1)}, u32[]{:S(2)}, u32[]{:S(2)}) async-start(bf16[32,256,2,128]{3,1,2,0:T(8,128)(2,1)} %stack.2), calls=%async_computation | async-start | bytes 8388608 | tf_op jit(solution)/shard_map/all_to_all | solution.py:124
  124.8 177.8 %all-gather.14.cloned.1.call-start = ((), (), s32[]{:S(2)}) async-start(), calls=%async_computation.5 | async-start | bytes 4866048 | tf_op jit(solution)/shard_map/all_gather | solution.py:166
  125.4 251.7 %all-reduce.3.cloned.1.call-start = ((), (), s32[]{:S(2)}) async-start(), calls=%async_computation.6 | async-start | bytes 262144 | tf_op jit(solution)/shard_map/psum | solution.py:157
  193.5 3.8 copy-start.4
  193.5 3.8 copy-start.6
  200.2 16.2 %copy-start.2 = (pred[256,8192]{0,1:T(8,128)(4,1)S(1)}, pred[256,8192]{0,1:T(8,128)(4,1)}, u32[]{:S(2)}) copy-start(pred[256,8192]{0,1:T(8,128)(4,1)} %fusion.6) | copy-start | bytes 6291460
  248.9 16.0 %copy-start.5 = (bf16[512,256]{1,0:T(8,128)(2,1)S(1)}, bf16[512,256]{1,0:T(8,128)(2,1)}, u32[]{:S(2)}) copy-start(bf16[512,256]{1,0:T(8,128)(2,1)} %param.26) | copy-start | bytes 786436
  265.9 111.2 %copy-start.3 = (bf16[256,256]{1,0:T(8,128)(2,1)S(1)}, bf16[256,256]{1,0:T(8,128)(2,1)}, u32[]{:S(2)}) copy-start(bf16[256,256]{1,0:T(8,128)(2,1)} %copy.51) | copy-start | bytes 393220
  265.9 204.1 %all-reduce.5.cloned.1.call-start = ((), (), s32[]{:S(2)}) async-start(), calls=%async_computation.7 | async-start | bytes 4718592 | tf_op jit(solution)/shard_map/psum | solution.py:170
  387.1 2.7 copy-start.9
Sparse Core Ops, SparseCore 0:
  9.9 51.6 all-gather.9
  64.1 48.3 all-gather.5
  115.0 78.4 all-gather.7
  195.8 53.0 all-gather.11
  251.3 51.2 all-gather.13
  304.8 72.2 all-reduce.2
  387.3 82.6 all-reduce.4
